TPU v7x, 512 devices: a whole 4x8x8 slice. The times are simulated.
512 devices in a mesh: bulk: 128 (over y, z, core), rep: 4 (over x).
Axes of the slice: x: 4, y: 8, z: 8, core: 2. Of those that a mesh axis runs over, the one named last changes fastest.
Arguments:
- orbitals: float32 [16384, 2048], P('rep', 'bulk'), may hold values from -6 to 6
- triangles: float32 [1024, 1024], P('rep', 'bulk'), may hold values from -0.09375 to 0.09375
- coupling: float32 [1024, 1024], P('rep', 'bulk'), may hold values from -0.09375 to 0.09375
- diagonals: float32 [2, 1024], P(None, 'bulk'), may hold values from 1 to 2
Outputs:
- solved: float32 [16384, 2048], P(('rep', 'bulk'))
All inputs are finite; a program needn't handle non-finite values.
Results may differ from a plain program's by a relative error of at most 0.000084.
Values sent between devices are 32-bit elements; how exact they have to be, the bound alone decides.
A program may use at most 64 MiB of HBM per device.

v0:
```python
import jax
import jax.numpy as jnp
from jax import lax
from jax.sharding import PartitionSpec as P


def unpack(triangles, diagonals):
    first_block = jnp.tril(triangles, -1) + jnp.diag(diagonals[0])
    second_block = jnp.tril(triangles.T, -1) + jnp.diag(diagonals[1])
    return (first_block, second_block)


def per_device(orbitals, triangles, coupling, diagonals):
    tri_rows, couple_rows = (
        lax.all_gather(triangles, "rep", axis=0, tiled=True),
        lax.all_gather(coupling, "rep", axis=0, tiled=True),
    )
    tri_whole, couple_whole, diag_whole = (
        lax.all_gather(tri_rows, "bulk", axis=1, tiled=True),
        lax.all_gather(couple_rows, "bulk", axis=1, tiled=True),
        lax.all_gather(diagonals, "bulk", axis=1, tiled=True),
    )
    first_block, second_block = unpack(tri_whole, diag_whole)
    panel = first_block.shape[0]
    groups = lax.axis_size("bulk")
    local_rows = orbitals.shape[0] // groups
    blocks = orbitals.reshape(groups, local_rows, orbitals.shape[1])
    received = lax.all_to_all(blocks, "bulk", split_axis=0, concat_axis=2, tiled=True)
    count = received.shape[1]
    full_width = received.shape[2]
    rows_now = received.reshape(count, full_width)
    left_part = rows_now[:, :panel]
    right_part = rows_now[:, panel:]
    solved_one = jax.scipy.linalg.solve_triangular(first_block, left_part.T, lower=True).T
    update = jnp.dot(
        solved_one,
        couple_whole.T,
        precision=lax.Precision.HIGHEST,
        preferred_element_type=jnp.float32,
    )
    solved_two = jax.scipy.linalg.solve_triangular(
        second_block, (right_part - update).T, lower=True
    ).T
    joined = jnp.concatenate([solved_one, solved_two], axis=1)
    result = joined.reshape(1, count, full_width)
    return result.reshape(local_rows, result.shape[2])


def solution(mesh):
    return jax.shard_map(
        per_device,
        mesh=mesh,
        in_specs=(P("rep", "bulk"), P("rep", "bulk"), P("rep", "bulk"), P(None, "bulk")),
        out_specs=P(("rep", "bulk"), None),
        check_vma=False,
    )
```

profile of v0, /device:TPU:1, one launch (start us, length us, event | category | flops | bytes accessed | tf_op | source)
XLA Modules:
  0.0 365.9 jit_solution(3939326885254710032)
XLA Ops:
  6.5 11.9 %all_gather.15 = f32[1024,8]{0,1:T(8,128)} all-gather(f32[256,8]{0,1:T(8,128)} %param.7), channel_id=1, replica_groups=mesh['bulk'=128,'rep'=4] {'rep'}, dimensions={0}, use_global_device_ids=true | all-gather | bytes 40960 | tf_op jit(solution)/shard_map/all_gather | solution.py:15
  18.5 1.3 reshape.27
  20.4 1.2 reshape.53
  21.6 20.3 %all-to-all-start = ((f32[128,1,512]{2,1,0:T(1,128)}), f32[128,1,512]{2,1,0:T(1,128)S(1)}, u32[]{:S(2)}, u32[]{:S(2)}) async-start(f32[128,1,512]{2,1,0:T(1,128)} %reshape.53), calls=%async_computation | async-start | bytes 524288 | tf_op jit(solution)/shard_map/all_to_all | solution.py:28
  41.9 10.3 %all_gather.18 = f32[1024,8]{0,1:T(8,128)} all-gather(f32[256,8]{0,1:T(8,128)S(1)} %copy-done.1), channel_id=1, replica_groups=mesh['bulk'=128,'rep'=4] {'rep'}, dimensions={0}, use_global_device_ids=true | all-gather | bytes 40960 | tf_op jit(solution)/shard_map/all_gather | solution.py:16
  53.1 53.9 %all-gather = f32[128,8,2]{1,2,0:T(2,128)S(1)} all-gather(f32[1,8,2]{1,2,0:T(2,128)S(1)} %bitcast.165), channel_id=1, replica_groups=mesh['bulk'=128,'rep'=4] {'bulk'}, dimensions={0}, use_global_device_ids=true | all-gather | bytes 8256 | tf_op jit(solution)/shard_map/all_gather | solution.py:21
  107.1 2.0 copy.25
  109.3 2.0 copy.26
  112.6 2.2 reduce
  115.1 1.1 fusion.71
  116.2 1.2 copy.30
  117.4 1.2 copy.29
  118.7 5.0 %add_select_fusion = f32[1024,1024]{0,1:T(8,128)} fusion(f32[1024,1024]{0,1:T(8,128)} %all-gather.4.cloned.1.call-done, f32[1024]{0:T(1024)S(1)} %bitcast.163, s32[1024]{0:T(1024)S(1)} %iota_add_fusion), kind=kLoop, calls=%fused_computation.9 | loop fusion | flops 7340032 | bytes 8396800 | tf_op jit(solution)/shard_map/jit(_solve_triangular)/triangular_solve | solution.py:34
  123.7 23.5 %while.4 = (s32[]{:T(128)}, f32[1024,1024]{0,1:T(8,128)}, s32[8,2]{0,1:T(2,128)S(1)}, f32[8,128,128]{2,1,0:T(8,128)S(1)}, s32[]{:T(128)}) while((s32[]{:T(128)}, f32[1024,1024]{0,1:T(8,128)}, s32[8,2]{0,1:T(2,128)S(1)}, f32[8,128,128]{2,1,0:T(8,128)S(1)}, s32[]{:T(128)}) %tuple.84), condition=%wide.while_cond, body=%wide.while_body.sunk | while | flops 2 | bytes 393329 | solution.py:34
  124.3 2.2 dynamic-slice.13
  127.2 2.2 dynamic-slice.13
  130.2 2.2 dynamic-slice.13
  133.1 2.2 dynamic-slice.13
  136.0 2.2 dynamic-slice.13
  139.0 2.2 dynamic-slice.13
  141.9 2.2 dynamic-slice.13
  144.9 2.1 dynamic-slice.13
  147.1 78.6 %custom-call.4 = f32[8,128,128]{1,2,0:T(8,128)S(1)} custom-call(f32[8,128,128]{2,1,0:T(8,128)S(1)} %get-tuple-element.20), custom_call_target="InvertDiagBlocksLowerTriangular" | custom-call | tf_op jit(solution)/shard_map/jit(_solve_triangular)/triangular_solve | solution.py:34
  225.7 5.1 %fusion.1 = f32[1024,1024]{1,0:T(8,128)} fusion(pred[1024,1024]{1,0:T(8,128)(4,1)S(1)} %copy.25, f32[1024,1024]{0,1:T(8,128)} %all-gather.4.cloned.1.call-done, pred[1024,1024]{1,0:T(8,128)(4,1)S(1)} %copy.26, f32[1024]{0:T(1024)S(1)} %bitcast.164), kind=kLoop, calls=%fused_computation.6 | loop fusion | flops 5242880 | bytes 10489856 | tf_op jit(solution)/shard_map/jit(_solve_triangular)/triangular_solve | solution.py:41
  230.8 23.2 %while.5 = (s32[]{:T(128)}, f32[1024,1024]{1,0:T(8,128)}, s32[8,2]{0,1:T(2,128)S(1)}, f32[8,128,128]{2,1,0:T(8,128)S(1)}, s32[]{:T(128)}) while((s32[]{:T(128)}, f32[1024,1024]{1,0:T(8,128)}, s32[8,2]{0,1:T(2,128)S(1)}, f32[8,128,128]{2,1,0:T(8,128)S(1)}, s32[]{:T(128)}) %tuple.94), condition=%wide.while_cond.clone, body=%wide.while_body.clone.sunk | while | flops 2 | bytes 131189 | solution.py:41
  231.5 2.3 bitcast_dynamic-update-slice_fusion.5
  234.4 2.3 bitcast_dynamic-update-slice_fusion.5
  237.3 2.3 bitcast_dynamic-update-slice_fusion.5
  240.2 2.3 bitcast_dynamic-update-slice_fusion.5
  243.1 2.3 bitcast_dynamic-update-slice_fusion.5
  246.0 2.3 bitcast_dynamic-update-slice_fusion.5
  248.9 2.3 bitcast_dynamic-update-slice_fusion.5
  251.8 2.2 bitcast_dynamic-update-slice_fusion.5
  254.1 78.8 %custom-call.5 = f32[8,128,128]{1,2,0:T(8,128)S(1)} custom-call(f32[8,128,128]{2,1,0:T(8,128)S(1)} %get-tuple-element.21), custom_call_target="InvertDiagBlocksLowerTriangular" | custom-call | tf_op jit(solution)/shard_map/jit(_solve_triangular)/triangular_solve | solution.py:41
  334.3 1.1 convolution_subtract_fusion.7
  335.5 1.2 convolution_subtract_fusion.6
  336.9 1.2 convolution_subtract_fusion.5
  338.3 1.3 convolution_subtract_fusion.14
  339.8 1.3 convolution_subtract_fusion.13
  341.3 1.4 convolution_subtract_fusion.12
  342.9 4.7 %fusion.2 = f32[1024,32]{0,1:T(8,128)S(1)} fusion(f32[32,1024]{1,0:T(8,128)S(1)} %copy.30, f32[1024,32]{0,1:T(8,128)S(1)} %convolution_dynamic-update-slice_fusion.1, f32[1024,1024]{0,1:T(8,128)} %all-gather.6.cloned.1.call-done), kind=kOutput, calls=%fused_computation.13 | convolution fusion | flops 402685952 | bytes 4587520 | tf_op jit(solution)/shard_map/dot_general | solution.py:35
  347.8 1.0 convolution_subtract_fusion.4
  349.0 1.1 convolution_subtract_fusion.3
  350.3 1.3 convolution_subtract_fusion.2
  351.8 1.3 convolution_subtract_fusion.1
  353.3 1.4 convolution_subtract_fusion.11
  354.9 1.5 convolution_subtract_fusion.10
  356.5 1.6 convolution_subtract_fusion.9
  (92 shorter events, 18.5 us)
Async XLA Ops:
  6.5 35.3 %copy-start.1 = (f32[256,8]{0,1:T(8,128)S(1)}, f32[256,8]{0,1:T(8,128)}, u32[]{:S(2)}) copy-start(f32[256,8]{0,1:T(8,128)} %param.8) | copy-start | bytes 24580
  6.5 46.5 %copy-start.2 = (f32[2,8]{1,0:T(2,128)S(1)}, f32[2,8]{1,0:T(2,128)}, u32[]{:S(2)}) copy-start(f32[2,8]{1,0:T(2,128)} %param.9) | copy-start | bytes 196
  6.5 112.1 %all-gather.4.cloned.1.call-start = ((), (), s32[]{:S(2)}) async-start(), calls=%async_computation.1 | async-start | bytes 4227072 | tf_op jit(solution)/shard_map/all_gather | solution.py:19
  21.6 89.8 %all-to-all-start = ((f32[128,1,512]{2,1,0:T(1,128)}), f32[128,1,512]{2,1,0:T(1,128)S(1)}, u32[]{:S(2)}, u32[]{:S(2)}) async-start(f32[128,1,512]{2,1,0:T(1,128)} %reshape.53), calls=%async_computation | async-start | bytes 524288 | tf_op jit(solution)/shard_map/all_to_all | solution.py:28
  41.8 301.1 %all-gather.6.cloned.1.call-start = ((), (), s32[]{:S(2)}) async-start(), calls=%async_computation.2 | async-start | bytes 4227072 | tf_op jit(solution)/shard_map/all_gather | solution.py:20
  111.4 0.7 copy-start
Sparse Core Ops, SparseCore 0:
  18.6 93.3 all-gather.3
  115.1 82.0 all-gather.5
where the time goes:
time: 368 us; the launch traced here: 366 us
  other arithmetic  171 us (46%)
  blocking collectives  76.1 us (21%)
  local copies, waits for them, and re-layouts  58.5 us (16%)
  matrix products  25.1 us (7%)
  starting transfers between devices  20.3 us (6%)
  between operations  13.8 us (4%)
    another operation x2, other arithmetic, per_device(): jax.scipy.linalg.solve_triangular(second_block, (right_part - update).T,...  83.9 us
    another operation x3, other arithmetic, per_device(): jax.scipy.linalg.solve_triangular(first_block, left_part.T, lower=True)  83.5 us
    all_gather x1, blocking collectives, per_device(): lax.all_gather(diagonals, 'bulk', axis=1, tiled=True)  53.9 us
    another operation x43, local copies, waits for them, and re-layouts, per_device(): jax.scipy.linalg.solve_triangular(first_block, left_part.T, lower=True)  23.3 us
    another operation x24, local copies, waits for them, and re-layouts, per_device(): jax.scipy.linalg.solve_triangular(second_block, (right_part - update).T,...  23.1 us
    all_to_all x1, starting transfers between devices, per_device(): lax.all_to_all(blocks, 'bulk', split_axis=0, concat_axis=2, tiled=True)  20.3 us
    all_gather x1, blocking collectives, per_device(): lax.all_gather(triangles, 'rep', axis=0, tiled=True)  11.9 us
    another operation x15, matrix products, per_device(): jax.scipy.linalg.solve_triangular(second_block, (right_part - update).T,...  10.6 us
  transfers between devices with their start and end apart: 3, of which 0 were waited for; matrix products, arithmetic and copies ran while one was open for 65% of the time, Pallas kernels for 0%

commit v1 on v0

v1 whole, which is shorter than its diff:
```python
import functools

import jax
import jax.numpy as jnp
from jax import lax
from jax.experimental import pallas as pl
from jax.experimental.pallas import tpu as pltpu
from jax.sharding import PartitionSpec as P

F32 = jnp.float32
BF16 = jnp.bfloat16
BLK = 256
BASE = 16


def split(a):
    hi = a.astype(BF16)
    lo = (a - hi.astype(F32)).astype(BF16)
    return hi, lo


def dot(a, b, transposed=False):
    dims = (((1,), (1 if transposed else 0,)), ((), ()))
    return lax.dot_general(a, b, dims, preferred_element_type=F32)


def product(a, b):
    (ah, al), (bh, bl) = a, b
    return dot(ah, bh) + (dot(ah, bl) + dot(al, bh))


def thin_product(x, bh, bl, transposed=False):
    xh, xl = split(x)
    rows = x.shape[0]
    both = dot(jnp.concatenate([xh, xl], axis=0), bh, transposed)
    return both[:rows] + (both[rows:] + dot(xh, bl, transposed))


def unit_upper_inverses(mats):
    size = mats[0].shape[0]
    row = lax.broadcasted_iota(jnp.int32, (size, size), 0)
    col = lax.broadcasted_iota(jnp.int32, (size, size), 1)
    same = (row // BASE) == (col // BASE)
    power = [jnp.where(same, -n, 0.0) for n in mats]
    eye = jnp.where(row == col, 1.0, 0.0)
    inv = [eye + p for p in power]
    span = 2
    while span < BASE:
        power = [product(split(p), split(p)) for p in power]
        inv = [m + product(split(m), split(p)) for m, p in zip(inv, power)]
        span *= 2
    width = BASE
    while width < size:
        corner = ((row // width) % 2 == 0) & ((col // width) == (row // width) + 1)
        parts = [split(m) for m in inv]
        corners = [product(split(jnp.where(corner, n, 0.0)), m) for n, m in zip(mats, parts)]
        inv = [m - product(ms, split(c)) for m, ms, c in zip(inv, parts, corners)]
        width *= 2
    return inv


def solve_kernel(tri_ref, couple_ref, orb_ref, diag_ref, out_ref, mh_ref, ml_ref):
    panel = 1024
    count = panel // BLK
    row = lax.broadcasted_iota(jnp.int32, (BLK, BLK), 0)
    col = lax.broadcasted_iota(jnp.int32, (BLK, BLK), 1)
    upper = row < col

    for k in range(count):
        cut = pl.ds(BLK * k, BLK)
        block = tri_ref[k, cut, :]
        one = jnp.where(upper, block, 0.0) / diag_ref[0:1, cut]
        two = jnp.where(upper, block.T, 0.0) / diag_ref[1:2, cut]
        for which, m in enumerate(unit_upper_inverses([one, two])):
            mh_ref[which, k], ml_ref[which, k] = split(m)

    left = [orb_ref[:, pl.ds(BLK * k, BLK)] for k in range(count)]
    right = [orb_ref[:, pl.ds(panel + BLK * k, BLK)] for k in range(count)]
    for k in range(count):
        cut = pl.ds(BLK * k, BLK)
        x = thin_product(left[k] / diag_ref[0:1, cut], mh_ref[0, k], ml_ref[0, k])
        out_ref[:, cut] = x
        for i in range(k + 1, count):
            left[i] = left[i] - thin_product(x, *split(tri_ref[i, cut, :]))
        for i in range(count):
            right[i] = right[i] - thin_product(x, *split(couple_ref[i, cut, :]))
    for k in range(count):
        cut = pl.ds(BLK * k, BLK)
        x = thin_product(right[k] / diag_ref[1:2, cut], mh_ref[1, k], ml_ref[1, k])
        out_ref[:, pl.ds(panel + BLK * k, BLK)] = x
        for i in range(k + 1, count):
            tri = tri_ref[k, pl.ds(BLK * i, BLK), :]
            right[i] = right[i] - thin_product(x, *split(tri), transposed=True)


def solve(tri, couple, orb, diag):
    rows = orb.shape[0]
    vmem = pl.BlockSpec(memory_space=pltpu.VMEM)
    return pl.pallas_call(
        solve_kernel,
        out_shape=jax.ShapeDtypeStruct((rows, 2048), F32),
        in_specs=[vmem] * 4,
        out_specs=vmem,
        scratch_shapes=[pltpu.VMEM((2, 4, BLK, BLK), BF16), pltpu.VMEM((2, 4, BLK, BLK), BF16)],
        compiler_params=pltpu.CompilerParams(vmem_limit_bytes=48 << 20),
        name="solve",
    )(tri, couple, orb, diag)


def per_device(orbitals, triangles, coupling, diagonals):
    groups = lax.axis_size("bulk")
    diag_rows = jnp.pad(diagonals, ((0, 6), (0, 248)))
    mine = jnp.concatenate([triangles.T, coupling.T, diag_rows], axis=0)
    whole = lax.all_gather(mine, ("rep", "bulk"))
    whole = whole.reshape(4, groups, 24, 256)
    tri = whole[:, :, 0:8].reshape(4, 1024, 256)
    couple = whole[:, :, 8:16].reshape(4, 1024, 256)
    diag = whole[0, :, 16:18, 0:8].transpose(1, 0, 2).reshape(2, 1024)
    local_rows = orbitals.shape[0] // groups
    blocks = orbitals.reshape(groups, local_rows, orbitals.shape[1])
    received = lax.all_to_all(blocks, "bulk", split_axis=0, concat_axis=2, tiled=True)
    orb = received.reshape(local_rows, 2048)
    return solve(tri, couple, orb, diag)


def solution(mesh):
    return jax.shard_map(
        per_device,
        mesh=mesh,
        in_specs=(P("rep", "bulk"), P("rep", "bulk"), P("rep", "bulk"), P(None, "bulk")),
        out_specs=P(("rep", "bulk"), None),
        check_vma=False,
    )
```

time: 368 us -> 190 us (0.52)
  other arithmetic: 171 us -> 2.64 us
  waiting for transfers between devices: 0.07 us -> 104 us
  local copies, waits for them, and re-layouts: 58.5 us -> 14.1 us
  blocking collectives: 76.1 us -> 32.5 us
  matrix products: 25.1 us -> 0 us
  Pallas kernels: 0 us -> 22.9 us
  starting transfers between devices: 20.3 us -> 0.01 us
    another operation x5 -> x0, other arithmetic: 167 us -> none  [the longest x2 83.9 us: per_device(): jax.scipy.linalg.solve_triangular(second_block, (right_part - update).T,...]
    all_gather x2 -> x1, waiting for transfers between devices: 0.03 us -> 104 us  [per_device(): whole = lax.all_gather(mine, ('rep', 'bulk'))]
    all_gather x3 -> x0, blocking collectives: 76.1 us -> none  [the longest x1 53.9 us: per_device(): lax.all_gather(diagonals, 'bulk', axis=1, tiled=True)]
    another operation x67 -> x0, local copies, waits for them, and re-layouts: 46.3 us -> none  [the longest x43 23.3 us: per_device(): jax.scipy.linalg.solve_triangular(first_block, left_part.T, lower=True)]
    all_to_all x0 -> x1, blocking collectives: none -> 32.5 us  [per_device(): lax.all_to_all(blocks, 'bulk', split_axis=0, concat_axis=2, tiled=True)]
    pallas_call x0 -> x1, Pallas kernels: none -> 22.9 us  [solve(): pl.pallas_call(solve_kernel, out_shape=jax.ShapeDtypeStruct((rows, 2048),...]
    another operation x30 -> x0, matrix products: 20.5 us -> none  [the longest x15 10.6 us: per_device(): jax.scipy.linalg.solve_triangular(second_block, (right_part - update).T,...]
    all_to_all x1 -> x0, starting transfers between devices: 20.3 us -> none  [per_device(): lax.all_to_all(blocks, 'bulk', split_axis=0, concat_axis=2, tiled=True)]
  transfers between devices with their start and end apart: 3 -> 1, of which waited for: 0 -> 1; matrix products, arithmetic and copies ran while one was open for 65% -> 3% of each run, Pallas kernels for 0% -> 0%
where the time goes in v1:
time: 190 us; the launch traced here: 189 us
  waiting for transfers between devices  104 us (55%)
  blocking collectives  32.5 us (17%)
  Pallas kernels  22.9 us (12%)
  local copies, waits for them, and re-layouts  14.1 us (7%)
  between operations  13.5 us (7%)
  other arithmetic  2.64 us (1%)
    all_gather x1, waiting for transfers between devices, per_device(): whole = lax.all_gather(mine, ('rep', 'bulk'))  104 us
    all_to_all x1, blocking collectives, per_device(): lax.all_to_all(blocks, 'bulk', split_axis=0, concat_axis=2, tiled=True)  32.5 us
    pallas_call x1, Pallas kernels, solve(): pl.pallas_call(solve_kernel, out_shape=jax.ShapeDtypeStruct((rows, 2048),...  22.9 us
    reshape x1, local copies, waits for them, and re-layouts, per_device(): couple = whole[:, :, 8:16].reshape(4, 1024, 256)  7.21 us
  transfers between devices with their start and end apart: 1, of which 1 were waited for; matrix products, arithmetic and copies ran while one was open for 3% of the time, Pallas kernels for 0%

profile of v1, /device:TPU:1, one launch (start us, length us, event | category | flops | bytes accessed | tf_op | source)
XLA Modules:
  0.0 189.4 jit_solution(10423385737900114925)
XLA Ops:
  6.5 0.0 all-gather.3.cloned.1.call-start
  6.5 1.3 select_maximum_fusion
  7.9 0.0 all-gather.3.cloned.1.call-update
  7.9 1.3 reshape.22
  9.2 0.6 copy.17
  9.8 0.5 reshape.27
  10.3 32.5 %all_to_all.15 = f32[128,1,512]{2,1,0:T(1,128)S(1)} all-to-all(f32[128,1,512]{2,1,0:T(1,128)S(1)} %reshape.27), channel_id=1, replica_groups=mesh['bulk'=128,'rep'=4] {'bulk'}, dimensions={0} | all-to-all | bytes 524288 | tf_op jit(solution)/shard_map/all_to_all | solution.py:121
  42.8 0.6 broadcast.6
  43.4 1.3 reduce
  44.7 0.3 reshape.28
  45.0 0.3 copy.12.orb_ref
  45.3 103.8 %all-gather.3.cloned.1.call-done = f32[12288,256]{1,0:T(8,128)} async-done(((f32[24,256]{1,0:T(8,128)}), f32[12288,256]{1,0:T(8,128)}) %all-gather.3.cloned.1.call-update) | async-done | bytes 12582928 | tf_op jit(solution)/shard_map/all_gather | solution.py:114
  149.1 7.2 %slice_bitcast_fusion = (f32[4,1024,256]{2,1,0:T(8,128)}, f32[4,1024,256]{2,1,0:T(8,128)}) fusion(f32[4,128,24,256]{3,2,1,0:T(8,128)} %bitcast.23), kind=kLoop, calls=%fused_computation | loop fusion | bytes 16777216 | tf_op jit(solution)/shard_map/reshape | solution.py:117
  156.3 1.1 slice.14
  157.4 0.1 reshape.24.diag_ref
  157.6 0.0 copy-start
  157.6 2.2 %copy-done = f32[4,1024,256]{2,1,0:T(8,128)S(1)} copy-done((f32[4,1024,256]{2,1,0:T(8,128)S(1)}, f32[4,1024,256]{2,1,0:T(8,128)}, u32[]{:S(2)}) %copy-start) | copy-done | bytes 4194328
  159.7 22.9 %solve.1 = f32[32,2048]{1,0:T(8,128)} custom-call(f32[4,1024,256]{2,1,0:T(8,128)S(1)} %copy-done, f32[4,1024,256]{2,1,0:T(8,128)} %get-tuple-element.5.couple_ref, f32[32,2048]{1,0:T(8,128)S(1)} %copy.12.orb_ref, f32[2,1024]{1,0:T(2,128)S(1)} %reshape.24.diag_ref), custom_call_target="tpu_custom_call" | custom-call | tf_op jit(solution)/shard_map/solve/pallas_call | solution.py:99
  (1 shorter events, 0.0 us)
Async XLA Ops:
  6.5 142.6 %all-gather.3.cloned.1.call-start = ((), (), s32[]{:S(2)}) async-start(), calls=%async_computation.1 | async-start | bytes 12607488 | tf_op jit(solution)/shard_map/all_gather | solution.py:114
  157.6 2.2 %copy-start = (f32[4,1024,256]{2,1,0:T(8,128)S(1)}, f32[4,1024,256]{2,1,0:T(8,128)}, u32[]{:S(2)}) copy-start(f32[4,1024,256]{2,1,0:T(8,128)} %get-tuple-element.6.tri_ref) | copy-start | bytes 12582916
Sparse Core Ops, SparseCore 0:
  12.0 137.0 all-gather.2

commit v2 on v1

v2 whole, which is shorter than its diff:
```python
import functools

import jax
import jax.numpy as jnp
from jax import lax
from jax.experimental import pallas as pl
from jax.experimental.pallas import tpu as pltpu
from jax.sharding import PartitionSpec as P

F32 = jnp.float32
BF16 = jnp.bfloat16
BLK = 256
BASE = 16
MESH = pl.DeviceIdType.MESH
NX, NY, NZ = 4, 8, 8
COPIES = 320


def split(a):
    hi = a.astype(BF16)
    lo = (a - hi.astype(F32)).astype(BF16)
    return hi, lo


def dot(a, b, transposed=False):
    dims = (((1,), (1 if transposed else 0,)), ((), ()))
    return lax.dot_general(a, b, dims, preferred_element_type=F32)


def product(a, b):
    (ah, al), (bh, bl) = a, b
    return dot(ah, bh) + (dot(ah, bl) + dot(al, bh))


def thin_product(x, bh, bl, transposed=False):
    xh, xl = split(x)
    rows = x.shape[0]
    both = dot(jnp.concatenate([xh, xl], axis=0), bh, transposed)
    return both[:rows] + (both[rows:] + dot(xh, bl, transposed))


def unit_upper_inverses(mats):
    size = mats[0].shape[0]
    row = lax.broadcasted_iota(jnp.int32, (size, size), 0)
    col = lax.broadcasted_iota(jnp.int32, (size, size), 1)
    same = (row // BASE) == (col // BASE)
    power = [jnp.where(same, -n, 0.0) for n in mats]
    eye = jnp.where(row == col, 1.0, 0.0)
    inv = [eye + p for p in power]
    span = 2
    while span < BASE:
        power = [product(split(p), split(p)) for p in power]
        inv = [m + product(split(m), split(p)) for m, p in zip(inv, power)]
        span *= 2
    width = BASE
    while width < size:
        corner = ((row // width) % 2 == 0) & ((col // width) == (row // width) + 1)
        parts = [split(m) for m in inv]
        corners = [product(split(jnp.where(corner, n, 0.0)), m) for n, m in zip(mats, parts)]
        inv = [m - product(ms, split(c)) for m, ms, c in zip(inv, parts, corners)]
        width *= 2
    return inv


def pack_kernel(orb_ref, tri_ref, couple_ref, diag_ref, mine_ref, diag_tile_ref, sent_ref):
    for half in range(2):
        cut = pl.ds(128 * half, 128)
        mine_ref[0, half] = tri_ref[:, cut]
        mine_ref[1, half] = couple_ref[:, cut]
    place = lax.axis_index("bulk") % 16
    lane = lax.broadcasted_iota(jnp.int32, (2, 128), 1)
    spread = jnp.concatenate([diag_ref[...]] * 16, axis=1)
    diag_tile_ref[...] = jnp.where(lane // 8 == place, spread, 0.0)
    group = lax.broadcasted_iota(jnp.int32, (8, 128), 1) // 16
    for g in range(4):
        stack = jnp.concatenate([orb_ref[:, pl.ds(128 * (8 * g + t), 128)] for t in range(8)], axis=0)
        turned = stack.T
        for p in range(2):
            pieces = [turned[64 * p + 8 * h : 64 * p + 8 * h + 8] for h in range(8)]
            for t in range(8):
                tile = jnp.zeros((8, 128), F32)
                for h in range(8):
                    moved = pieces[h] if h == t else pltpu.roll(pieces[h], (16 * (h - t)) % 128, 1)
                    tile = jnp.where(group == h, moved, tile)
                sent_ref[2 * (8 * g + t) + p] = tile


def pack(orbitals, triangles, coupling, diagonals):
    vmem = pl.BlockSpec(memory_space=pltpu.VMEM)
    return pl.pallas_call(
        pack_kernel,
        out_shape=(
            jax.ShapeDtypeStruct((2, 2, 8, 128), F32),
            jax.ShapeDtypeStruct((2, 128), F32),
            jax.ShapeDtypeStruct((NY * NZ, 8, 128), F32),
        ),
        in_specs=[vmem] * 4,
        out_specs=(vmem,) * 3,
        name="pack",
    )(orbitals, triangles, coupling, diagonals)


def ring_hops(n):
    return [(1, d) for d in range(1, n // 2 + 1)] + [(-1, d) for d in range(1, n - n // 2)]


class Copies:
    def __init__(self, send, recv):
        self.send, self.recv, self.count, self.started = send, recv, 0, []

    def slot(self):
        self.count += 1
        return self.count - 1

    def remote(self, src, dst, device):
        at = self.slot()
        copy = pltpu.make_async_remote_copy(
            src_ref=src, dst_ref=dst, send_sem=self.send.at[at], recv_sem=self.recv.at[at],
            device_id=device, device_id_type=MESH)
        copy.start()
        self.started.append(copy)
        return copy


def exchange_kernel(mine, diag_tile, sent, whole, diags, orbs, first, local, send, recv):
    bulk, x = lax.axis_index("bulk"), lax.axis_index("rep")
    c = lax.rem(bulk, 2)
    z = lax.rem(bulk // 2, NZ)
    y = bulk // (2 * NZ)
    s = 1 - 2 * c
    me = {"x": x, "y": y, "z": z}
    size = {"x": NX, "y": NY, "z": NZ}

    def shifted(axis, by):
        return lax.rem(me[axis] + by + 2 * size[axis], size[axis])

    def device(axis, by):
        at = dict(me)
        at[axis] = shifted(axis, by)
        return ((at["y"] * NZ + at["z"]) * 2 + c, at["x"])

    partner = (bulk + s, x)
    barrier = pltpu.get_barrier_semaphore()
    peers = [device(a, o) for a in "xyz" for o in range(1, size[a])] + [partner]
    for peer in peers:
        pl.semaphore_signal(barrier, inc=1, device_id=peer, device_id_type=MESH)
    pl.semaphore_wait(barrier, len(peers))

    copies = Copies(send, recv)
    keep = pltpu.make_async_copy(mine, whole.at[:, :, x, y, z, c], local.at[0])
    keep_diag = pltpu.make_async_copy(diag_tile, diags.at[y, z, c], local.at[1])
    keep_first = pltpu.make_async_copy(sent.at[y], first.at[y], local.at[2])
    for copy in (keep, keep_diag, keep_first):
        copy.start()

    lines = []
    for o in range(1, 8):
        for half, axis in ((0, "z"), (1, "y")):
            lines.append(copies.remote(mine.at[:, half], whole.at[:, half, x, y, z, c], device(axis, o)))
    diag_line = [copies.remote(diag_tile, diags.at[y, z, c], device("z", o)) for o in range(1, 8)]

    colours = [(1, 0, "z", "y", "x"), (1, 1, "y", "z", "x"), (0, 0, "z", "x", "y"), (0, 1, "y", "x", "z")]

    def block(colour, index):
        t, half, line, _, _ = colour
        at = {**me, **index}
        at[line] = slice(None)
        return whole.at[t, half, at["x"], at["y"], at["z"], c]

    events = {}

    def later(slot, action):
        events.setdefault(slot, []).append(action)

    def to_partner(ref):
        crossing.append(copies.remote(ref, ref, partner))

    crossing = []

    def start_ring(colour, axis, index, slot, arrived):
        n = size[axis]
        hops = ring_hops(n)
        own = block(colour, {**index, axis: me[axis]})
        coming = {}
        for way in (1, -1):
            coming[way, 1] = copies.remote(own, own, device(axis, way * s))
        for way, d in sorted(hops, key=lambda h: h[1]):
            def action(way=way, d=d):
                coming[way, d].wait_recv()
                at = shifted(axis, -way * s * d)
                ref = block(colour, {**index, axis: at})
                if (way, d + 1) in hops:
                    coming[way, d + 1] = copies.remote(ref, ref, device(axis, way * s))
                arrived(axis, at, slot + d)
            later(slot + d, action)

    def final_arrival(colour, index):
        def arrived(axis, at, slot):
            to_partner(block(colour, {**index, axis: at}))
        return arrived

    def middle_arrival(colour):
        def arrived(axis, at, slot):
            start_ring(colour, colour[4], {axis: at}, slot, final_arrival(colour, {axis: at}))
            to_partner(block(colour, {axis: at}))
        return arrived

    for copy in lines:
        copy.wait_recv()
    keep.wait()
    for colour in colours:
        start_ring(colour, colour[3], {}, 0, middle_arrival(colour))
    for colour in colours:
        start_ring(colour, colour[4], {}, 0, final_arrival(colour, {}))
    for colour in colours:
        to_partner(block(colour, {}))

    keep_first.wait()
    turned = [copies.remote(sent.at[shifted("y", o)], first.at[y], device("y", o)) for o in range(1, 8)]

    def diag_second():
        for copy in diag_line:
            copy.wait_recv()
        keep_diag.wait()
        diag_blocks.extend(
            copies.remote(diags.at[y, :, c], diags.at[y, :, c], device("y", o)) for o in range(1, 8))

    def orbital_second():
        for copy in turned:
            copy.wait_recv()
        keep_second = pltpu.make_async_copy(first.at[:, z], orbs.at[c, z], local.at[3])
        keep_second.start()
        orbital_blocks.extend(
            copies.remote(first.at[:, shifted("z", o)], orbs.at[c, z], device("z", o)) for o in range(1, 8))
        keep_second.wait()

    def diag_last():
        for copy in diag_blocks:
            copy.wait_recv()
        to_partner(diags.at[:, :, c])

    def orbital_last():
        for copy in orbital_blocks:
            copy.wait_recv()
        to_partner(orbs.at[c])

    diag_blocks, orbital_blocks = [], []
    later(1, diag_second)
    later(2, orbital_second)
    later(3, diag_last)
    later(5, orbital_last)
    slot = 0
    while slot <= max(events):
        for action in events.get(slot, []):
            action()
        slot += 1
    for copy in crossing:
        copy.wait_recv()
    for copy in copies.started:
        copy.wait_send()


def exchange(mine, diag_tile, sent):
    anywhere = pl.BlockSpec(memory_space=pl.ANY)
    vmem = pl.BlockSpec(memory_space=pltpu.VMEM)
    return pl.pallas_call(
        exchange_kernel,
        out_shape=(
            jax.ShapeDtypeStruct((2, 2, NX, NY, NZ, 2, 8, 128), F32),
            jax.ShapeDtypeStruct((NY, NZ, 2, 2, 128), F32),
            jax.ShapeDtypeStruct((2, NZ, NY, 8, 128), F32),
        ),
        in_specs=[vmem] * 3,
        out_specs=(anywhere,) * 3,
        scratch_shapes=[
            pltpu.VMEM((NY, NZ, 8, 128), F32),
            pltpu.SemaphoreType.DMA((4,)),
            pltpu.SemaphoreType.DMA((COPIES,)),
            pltpu.SemaphoreType.DMA((COPIES,)),
        ],
        compiler_params=pltpu.CompilerParams(collective_id=0, has_side_effects=True),
        name="exchange",
    )(mine, diag_tile, sent.reshape(NY, NZ, 8, 128))


def solve_kernel(whole_ref, diags_ref, orbs_ref, out_ref, mh_ref, ml_ref):
    panel = 1024
    count = panel // BLK
    row = lax.broadcasted_iota(jnp.int32, (BLK, BLK), 0)
    col = lax.broadcasted_iota(jnp.int32, (BLK, BLK), 1)
    upper = row < col

    def factor(t, i, j):
        cut = pl.ds(BLK * j, BLK)
        return jnp.concatenate([whole_ref[t, 0, i, cut, :], whole_ref[t, 1, i, cut, :]], axis=1)

    scales = []
    for which in range(2):
        rows = [jnp.sum(diags_ref[w, :, which, :], axis=0, keepdims=True) for w in range(8)]
        scales.append([1.0 / jnp.concatenate(rows[2 * k : 2 * k + 2], axis=1) for k in range(count)])

    for k in range(count):
        block = factor(0, k, k)
        one = jnp.where(upper, block, 0.0) * scales[0][k]
        two = jnp.where(upper, block.T, 0.0) * scales[1][k]
        for which, m in enumerate(unit_upper_inverses([one, two])):
            mh_ref[which, k], ml_ref[which, k] = split(m)

    odd = lax.axis_index("bulk") % 2 == 1
    group = lax.broadcasted_iota(jnp.int32, (8, 128), 1) // 16
    columns = []
    for w in range(16):
        tiles = [orbs_ref[e % 2, 4 * (w % 2) + e // 2, w // 2] for e in range(8)]
        tiles = [jnp.where(odd, pltpu.roll(t, 64, 1), t) for t in tiles]
        strips = []
        for h in range(4):
            strip = jnp.zeros((8, 128), F32)
            for e in range(8):
                moved = tiles[e] if e == h else pltpu.roll(tiles[e], (16 * (e - h)) % 128, 1)
                strip = jnp.where(group == e, moved, strip)
            strips.append(strip)
        columns.append(jnp.concatenate(strips, axis=0))
    blocks = [jnp.concatenate(columns[2 * k : 2 * k + 2], axis=1) for k in range(2 * count)]
    left, right = blocks[:count], blocks[count:]

    for k in range(count):
        x = thin_product(left[k] * scales[0][k], mh_ref[0, k], ml_ref[0, k])
        out_ref[:, pl.ds(BLK * k, BLK)] = x
        for i in range(k + 1, count):
            left[i] = left[i] - thin_product(x, *split(factor(0, i, k)))
        for i in range(count):
            right[i] = right[i] - thin_product(x, *split(factor(1, i, k)))
    for k in range(count):
        x = thin_product(right[k] * scales[1][k], mh_ref[1, k], ml_ref[1, k])
        out_ref[:, pl.ds(panel + BLK * k, BLK)] = x
        for i in range(k + 1, count):
            right[i] = right[i] - thin_product(x, *split(factor(0, k, i)), transposed=True)


def solve(whole, diags, orbs):
    vmem = pl.BlockSpec(memory_space=pltpu.VMEM)
    return pl.pallas_call(
        solve_kernel,
        out_shape=jax.ShapeDtypeStruct((32, 2048), F32),
        in_specs=[vmem] * 3,
        out_specs=vmem,
        scratch_shapes=[pltpu.VMEM((2, 4, BLK, BLK), BF16), pltpu.VMEM((2, 4, BLK, BLK), BF16)],
        compiler_params=pltpu.CompilerParams(vmem_limit_bytes=32 << 20),
        name="solve",
    )(whole.reshape(2, 2, NX, 1024, 128), diags.reshape(8, 16, 2, 128), orbs)


def per_device(orbitals, triangles, coupling, diagonals):
    mine, diag_tile, sent = pack(orbitals.T, triangles.T, coupling.T, diagonals)
    return solve(*exchange(mine, diag_tile, sent))


def solution(mesh):
    return jax.shard_map(
        per_device,
        mesh=mesh,
        in_specs=(P("rep", "bulk"), P("rep", "bulk"), P("rep", "bulk"), P(None, "bulk")),
        out_specs=P(("rep", "bulk"), None),
        check_vma=False,
    )
```

time: 190 us -> 93.3 us (0.49)
  waiting for transfers between devices: 104 us -> 0 us
  Pallas kernels: 22.9 us -> 87.7 us
  blocking collectives: 32.5 us -> 0 us
  between operations: 13.5 us -> 0.02 us
  local copies, waits for them, and re-layouts: 14.1 us -> 5.32 us
  other arithmetic: 2.64 us -> 0 us
    all_gather x1 -> x0, waiting for transfers between devices: 104 us -> none  [per_device(): whole = lax.all_gather(mine, ('rep', 'bulk'))]
    pallas_call x1 -> x3, Pallas kernels: 22.9 us -> 87.7 us  [the longest x1 64.6 us: exchange(): pl.pallas_call(exchange_kernel, out_shape=(jax.ShapeDtypeStruct((2, 2, NX...]
    all_to_all x1 -> x0, blocking collectives: 32.5 us -> none  [per_device(): lax.all_to_all(blocks, 'bulk', split_axis=0, concat_axis=2, tiled=True)]
    reshape x5 -> x0, local copies, waits for them, and re-layouts: 9.54 us -> none  [the longest x1 7.21 us: per_device(): couple = whole[:, :, 8:16].reshape(4, 1024, 256)]
    unnamed x5 -> x6, local copies, waits for them, and re-layouts: 2.91 us -> 5.32 us
  transfers between devices with their start and end apart: 1 -> 0, of which waited for: 1 -> 0; matrix products, arithmetic and copies ran while one was open for 3% -> 0% of each run, Pallas kernels for 0% -> 0%
where the time goes in v2:
time: 93.3 us; the launch traced here: 93 us
  Pallas kernels  87.7 us (94%)
  local copies, waits for them, and re-layouts  5.32 us (6%)
    pallas_call x1, Pallas kernels, exchange(): pl.pallas_call(exchange_kernel, out_shape=(jax.ShapeDtypeStruct((2, 2, NX...  64.6 us
    pallas_call x1, Pallas kernels, solve(): pl.pallas_call(solve_kernel, out_shape=jax.ShapeDtypeStruct((32, 2048), F...  20.7 us
    unnamed x6, local copies, waits for them, and re-layouts  5.32 us
    pallas_call x1, Pallas kernels, pack(): pl.pallas_call(pack_kernel, out_shape=(jax.ShapeDtypeStruct((2, 2, 8, 128...  2.32 us

profile of v2, /device:TPU:1, one launch (start us, length us, event | category | flops | bytes accessed | tf_op | source)
XLA Modules:
  0.0 93.0 jit_solution(12439426792809784813)
XLA Ops:
  0.0 2.3 %pack.1 = (f32[2,2,8,128]{3,2,1,0:T(8,128)}, f32[2,128]{1,0:T(2,128)}, f32[64,8,128]{2,1,0:T(8,128)}) custom-call(f32[16,4096]{1,0:T(8,128)} %bitcast.8, f32[8,256]{1,0:T(8,128)} %bitcast.10, f32[8,256]{1,0:T(8,128)} %bitcast.11, f32[2,8]{1,0:T(2,128)} %diag_ref.1), custom_call_target="tpu_custom_call" | custom-call | tf_op jit(solution)/shard_map/pack/pallas_call | solution.py:90
  2.3 64.6 %exchange.1 = (f32[2,2,4,8,8,2,8,128]{7,6,5,4,3,2,1,0:T(8,128)}, f32[8,8,2,2,128]{4,3,2,1,0:T(2,128)}, f32[2,8,8,8,128]{4,3,2,1,0:T(8,128)}) custom-call(f32[2,2,8,128]{3,2,1,0:T(8,128)} %get-tuple-element.11.mine, f32[2,128]{1,0:T(2,128)} %get-tuple-element.12.diag_tile, f32[8,8,8,128]{3,2,1,0:T(8,128)} %bitcast.9), custom_call_target="tpu_custom_call" | custom-call | tf_op jit(solution)/shard_map/exchange/pallas_call | solution.py:266
  67.0 0.0 copy-start
  67.0 3.4 %copy-done = f32[2,2,4,8,8,2,8,128]{7,6,5,4,3,2,1,0:T(8,128)S(1)} copy-done((f32[2,2,4,8,8,2,8,128]{7,6,5,4,3,2,1,0:T(8,128)S(1)}, f32[2,2,4,8,8,2,8,128]{7,6,5,4,3,2,1,0:T(8,128)}, u32[]{:S(2)}) %copy-start) | copy-done | bytes 8388632
  70.3 0.0 copy-start.1
  70.4 1.0 %copy-done.1 = f32[2,8,8,8,128]{4,3,2,1,0:T(8,128)S(1)} copy-done((f32[2,8,8,8,128]{4,3,2,1,0:T(8,128)S(1)}, f32[2,8,8,8,128]{4,3,2,1,0:T(8,128)}, u32[]{:S(2)}) %copy-start.1) | copy-done | bytes 524312
  71.4 0.0 copy-start.2
  71.4 0.9 copy-done.2
  72.3 20.7 %solve.1 = f32[32,2048]{1,0:T(8,128)} custom-call(f32[2,2,4,1024,128]{4,3,2,1,0:T(8,128)S(1)} %bitcast.6, f32[8,16,2,128]{3,2,1,0:T(2,128)S(1)} %bitcast.7, f32[2,8,8,8,128]{4,3,2,1,0:T(8,128)S(1)} %copy-done.1), custom_call_target="tpu_custom_call" | custom-call | tf_op jit(solution)/shard_map/solve/pallas_call | solution.py:342
Async XLA Ops:
  67.0 3.4 %copy-start = (f32[2,2,4,8,8,2,8,128]{7,6,5,4,3,2,1,0:T(8,128)S(1)}, f32[2,2,4,8,8,2,8,128]{7,6,5,4,3,2,1,0:T(8,128)}, u32[]{:S(2)}) copy-start(f32[2,2,4,8,8,2,8,128]{7,6,5,4,3,2,1,0:T(8,128)} %get-tuple-element.14) | copy-start | bytes 25165828
  70.3 1.0 %copy-start.1 = (f32[2,8,8,8,128]{4,3,2,1,0:T(8,128)S(1)}, f32[2,8,8,8,128]{4,3,2,1,0:T(8,128)}, u32[]{:S(2)}) copy-start(f32[2,8,8,8,128]{4,3,2,1,0:T(8,128)} %get-tuple-element.16.orbs_ref) | copy-start | bytes 1572868
  71.4 0.9 copy-start.2

commit v3 on v1

v3 whole, which is shorter than its diff:
```python
import functools

import jax
import jax.numpy as jnp
from jax import lax
from jax.experimental import pallas as pl
from jax.experimental.pallas import tpu as pltpu
from jax.sharding import PartitionSpec as P

F32 = jnp.float32
BF16 = jnp.bfloat16
BLK = 256
BASE = 16
MESH = pl.DeviceIdType.MESH
NX, NY, NZ = 4, 8, 8
COPIES = 320


def split(a):
    hi = a.astype(BF16)
    lo = (a - hi.astype(F32)).astype(BF16)
    return hi, lo


def dot(a, b, transposed=False):
    dims = (((1,), (1 if transposed else 0,)), ((), ()))
    return lax.dot_general(a, b, dims, preferred_element_type=F32)


def product(a, b):
    (ah, al), (bh, bl) = a, b
    return dot(ah, bh) + (dot(ah, bl) + dot(al, bh))


def thin_product(x, bh, bl, transposed=False):
    xh, xl = split(x)
    rows = x.shape[0]
    both = dot(jnp.concatenate([xh, xl], axis=0), bh, transposed)
    return both[:rows] + (both[rows:] + dot(xh, bl, transposed))


def unit_upper_inverses(mats):
    size = mats[0].shape[0]
    row = lax.broadcasted_iota(jnp.int32, (size, size), 0)
    col = lax.broadcasted_iota(jnp.int32, (size, size), 1)
    same = (row // BASE) == (col // BASE)
    eye = jnp.where(row == col, 1.0, 0.0)
    power = [jnp.where(same, -n, 0.0) for n in mats]
    inv = [eye + p for p in power]
    span = 2
    while span < BASE:
        parts = [split(p) for p in power]
        power = [product(p, p) for p in parts]
        parts = [split(p) for p in power]
        inv = [m + product(split(m), p) for m, p in zip(inv, parts)]
        span *= 2
    width = BASE
    while width < size:
        corner = ((row // width) % 2 == 0) & ((col // width) == (row // width) + 1)
        parts = [split(m) for m in inv]
        corners = [product(split(jnp.where(corner, n, 0.0)), m) for n, m in zip(mats, parts)]
        inv = [m - product(ms, split(c)) for m, ms, c in zip(inv, parts, corners)]
        width *= 2
    return [split(m) for m in inv]


def ring_hops(n):
    return [(1, d) for d in range(1, n // 2 + 1)] + [(-1, d) for d in range(1, n - n // 2)]


def exchange_body(tri, couple, orb, diag, whole, diags, orbs, sent, first, diag_tile, diag_in, orb_in, local, send, recv, pack_work, invert, unpack):
    bulk, x = lax.axis_index("bulk"), lax.axis_index("rep")
    c = lax.rem(bulk, 2)
    z = lax.rem(bulk // 2, NZ)
    y = bulk // (2 * NZ)
    s = 1 - 2 * c
    me = {"x": x, "y": y, "z": z}
    size = {"x": NX, "y": NY, "z": NZ}
    used = {"send": 0, "recv": 0}

    def new(kind):
        used[kind] += 1
        return used[kind] - 1

    def shifted(axis, by):
        return lax.rem(me[axis] + by + 2 * size[axis], size[axis])

    def device(axis, by):
        at = dict(me)
        at[axis] = shifted(axis, by)
        return ((at["y"] * NZ + at["z"]) * 2 + c, at["x"])

    partner = (bulk + s, x)

    def put(src, dst, to, send_at, recv_at):
        pltpu.make_async_remote_copy(
            src_ref=src, dst_ref=dst, send_sem=send.at[send_at], recv_sem=recv.at[recv_at],
            device_id=to, device_id_type=MESH).start()

    def take(sem, ref):
        pltpu.make_async_copy(ref, ref, sem).wait()

    get_diag = pltpu.make_async_copy(diag, diag_in, local.at[0])
    get_orb = pltpu.make_async_copy(orb, orb_in, local.at[1])
    get_orb.start()
    get_diag.start()
    barrier = pltpu.get_barrier_semaphore()
    peers = [device(a, o) for a in "xyz" for o in range(1, size[a])] + [partner]
    for peer in peers:
        pl.semaphore_signal(barrier, inc=1, device_id=peer, device_id_type=MESH)
    keeps = []
    for t, ref in ((0, tri), (1, couple)):
        for half in range(2):
            keep = pltpu.make_async_copy(ref.at[:, pl.ds(128 * half, 128)], whole.at[t, half, x, y, z, c], local.at[2 + 2 * t + half])
            keep.start()
            keeps.append(keep)
    pl.semaphore_wait(barrier, len(peers))

    line_send = new("send")
    line_recv = {(t, half): new("recv") for t in range(2) for half in range(2)}
    order = (4, 3, 5, 2, 6, 1, 7)
    for t, ref in ((1, couple), (0, tri)):
        for o in order:
            for half, axis in ((0, "z"), (1, "y")):
                put(ref.at[:, pl.ds(128 * half, 128)], whole.at[t, half, x, y, z, c], device(axis, o), line_send, line_recv[t, half])

    pack_work(get_orb, get_diag)
    put_diag = pltpu.make_async_copy(diag_tile, diags.at[y, z, c], local.at[6])
    put_diag.start()
    keep_first = pltpu.make_async_copy(sent.at[y], first.at[y], local.at[7])
    keep_first.start()
    diag_send, diag_recv = new("send"), new("recv")
    for o in order:
        put(diag_tile, diags.at[y, z, c], device("z", o), diag_send, diag_recv)

    colours = [(1, 0, "z", "y", "x"), (1, 1, "y", "z", "x"), (0, 0, "z", "x", "y"), (0, 1, "y", "x", "z")]
    ring_send = {colour: (new("send"), new("send")) for colour in colours}
    cross_send = new("send")
    cross_recv = {colour: new("recv") for colour in colours}

    def block(colour, index):
        t, half, line, _, _ = colour
        at = {**me, **index}
        at[line] = slice(None)
        return whole.at[t, half, at["x"], at["y"], at["z"], c]

    def blocks_like(n):
        a = {1: (1, 1), 2: (2, 1), 7: (1, 7), 3: (3, 1), 24: (3, 8), 28: (4, 7), 32: (4, 8)}[n]
        return whole.at[0, 0, pl.ds(0, a[0]), pl.ds(0, a[1]), :, 0]

    events = {}

    def later(slot, action, rank=0):
        events.setdefault(slot, []).append((rank, len(events.get(slot, [])), action))

    crossings = []

    def to_partner(colour, ref):
        put(ref, ref, partner, cross_send, cross_recv[colour])
        crossings.append(colour)

    def final_ring(colour, indices, slot):
        axis = colour[4]
        n, hops = size[axis], ring_hops(size[axis])
        sems = {hop: new("recv") for hop in hops}
        for index in indices:
            own = block(colour, index)
            for way in (1, -1):
                put(own, own, device(axis, way * s), ring_send[colour][1], sems[way, 1])
            to_partner(colour, own)
        for way, d in sorted(hops, key=lambda h: h[1]):
            def action(way=way, d=d):
                take(recv.at[sems[way, d]], blocks_like(len(indices)))
                for index in indices:
                    ref = block(colour, {**index, axis: shifted(axis, -way * s * d)})
                    if (way, d + 1) in hops:
                        put(ref, ref, device(axis, way * s), ring_send[colour][1], sems[way, d + 1])
                    to_partner(colour, ref)
            later(slot + d, action, 1)

    def middle_ring(colour):
        axis = colour[3]
        n, hops = size[axis], ring_hops(size[axis])
        sems = {hop: new("recv") for hop in hops}
        own = block(colour, {})
        for way in (1, -1):
            put(own, own, device(axis, way * s), ring_send[colour][0], sems[way, 1])
        for d in range(1, n // 2 + 1):
            ways = [way for way in (1, -1) if (way, d) in hops]
            def action(d=d, ways=ways):
                indices = []
                for way in ways:
                    take(recv.at[sems[way, d]], blocks_like(1))
                    index = {axis: shifted(axis, -way * s * d)}
                    ref = block(colour, index)
                    if (way, d + 1) in hops:
                        put(ref, ref, device(axis, way * s), ring_send[colour][0], sems[way, d + 1])
                    indices.append(index)
                final_ring(colour, indices, d)
            later(d, action)

    for keep in keeps:
        keep.wait()
    for colour in colours:
        take(recv.at[line_recv[colour[0], colour[1]]], whole.at[0, 0, 0, 0, pl.ds(0, 7), 0])
        middle_ring(colour)
    for colour in colours:
        final_ring(colour, [{}], 0)

    first_send, first_recv, second_send, second_recv = new("send"), new("recv"), new("send"), new("recv")
    dblock_send, dblock_recv = new("send"), new("recv")
    cross_small = [(new("send"), new("recv")) for _ in range(2)]

    def orbital_first():
        keep_first.wait()
        for o in order:
            at = shifted("y", o)
            put(sent.at[at], first.at[y], device("y", o), first_send, first_recv)

    def orbital_second():
        take(recv.at[first_recv], first.at[pl.ds(0, 7)])
        keep_second = pltpu.make_async_copy(first.at[:, z], orbs.at[c, z], local.at[8])
        keep_second.start()
        for o in order:
            put(first.at[:, shifted("z", o)], orbs.at[c, z], device("z", o), second_send, second_recv)
        keep_second.wait()

    def orbital_last():
        take(recv.at[second_recv], orbs.at[0, pl.ds(0, 7)])
        put(orbs.at[c], orbs.at[c], partner, *cross_small[0])

    def diag_second():
        put_diag.wait()
        take(recv.at[diag_recv], diags.at[0, pl.ds(0, 7), 0])
        for o in order:
            put(diags.at[y, :, c], diags.at[y, :, c], device("y", o), dblock_send, dblock_recv)

    def diag_last():
        take(recv.at[dblock_recv], diags.at[pl.ds(0, 7), :, 0])
        put(diags.at[:, :, c], diags.at[:, :, c], partner, *cross_small[1])

    later(0, orbital_first, 2)
    later(2, orbital_second, 2)
    later(5, orbital_last, 2)
    later(1, diag_second, 2)
    later(3, diag_last, 2)
    def triangles_ready():
        take(recv.at[cross_small[1][1]], diags.at[:, :, 0])
        for colour in colours[2:]:
            take(recv.at[cross_recv[colour]], blocks_like(32))
        invert()

    def orbitals_ready():
        take(recv.at[cross_small[0][1]], orbs.at[0])
        unpack()

    later(6, triangles_ready, 5)
    later(6, orbitals_ready, 6)
    slot = 0
    while slot <= max(events):
        done = 0
        while done < len(events.get(slot, [])):
            todo = sorted(events[slot][done:])
            done += len(todo)
            for _, _, action in todo:
                action()
        slot += 1

    for colour in colours[:2]:
        take(recv.at[cross_recv[colour]], blocks_like(32))

    def finish():
        take(send.at[line_send], whole.at[:, :, 0, 0, pl.ds(0, 7), 0])
        take(send.at[diag_send], diags.at[0, pl.ds(0, 7), 0])
        for colour in colours:
            take(send.at[ring_send[colour][0]], blocks_like(7 if size[colour[3]] == 8 else 3))
            take(send.at[ring_send[colour][1]], blocks_like(24 if size[colour[4]] == 4 else 28))
        take(send.at[cross_send], whole.at[:, :, :, :, :, 0])
        take(send.at[first_send], first.at[pl.ds(0, 7)])
        take(send.at[second_send], orbs.at[0, pl.ds(0, 7)])
        take(send.at[dblock_send], diags.at[pl.ds(0, 7), :, 0])
        take(send.at[cross_small[0][0]], orbs.at[0])
        take(send.at[cross_small[1][0]], diags.at[:, :, 0])

    assert used["send"] <= SENDS and used["recv"] <= RECVS, used
    return finish


def pack_into(orb_in, diag_in, sent, diag_tile):
    place = lax.axis_index("bulk") % 16
    lane = lax.broadcasted_iota(jnp.int32, (2, 128), 1)
    spread = jnp.concatenate([diag_in[...]] * 16, axis=1)
    diag_tile[...] = jnp.where(lane // 8 == place, spread, 0.0)
    group = lax.broadcasted_iota(jnp.int32, (8, 128), 1) // 16
    for g in range(4):
        stack = jnp.concatenate([orb_in[:, pl.ds(128 * (8 * g + t), 128)] for t in range(8)], axis=0)
        turned = stack.T
        for p in range(2):
            pieces = [turned[64 * p + 8 * h : 64 * p + 8 * h + 8] for h in range(8)]
            for t in range(8):
                tile = jnp.zeros((8, 128), F32)
                for h in range(8):
                    moved = pieces[h] if h == t else pltpu.roll(pieces[h], (16 * (h - t)) % 128, 1)
                    tile = jnp.where(group == h, moved, tile)
                chip = 2 * (8 * g + t) + p
                sent[chip // NZ, chip % NZ] = tile


def exchange_kernel(tri, couple, orb, diag, out_ref, whole, diags, orbs, sent, first, diag_tile, diag_in, orb_in, mh_ref, ml_ref, local, send, recv):
    def pack_work(get_orb, get_diag):
        get_diag.wait()
        get_orb.wait()
        pack_into(orb_in, diag_in, sent, diag_tile)

    panel = 1024
    count = panel // BLK
    row = lax.broadcasted_iota(jnp.int32, (BLK, BLK), 0)
    col = lax.broadcasted_iota(jnp.int32, (BLK, BLK), 1)
    upper = row < col

    def factor(t, i, j):
        return jnp.concatenate([whole[t, half, i, 2 * j : 2 * j + 2].reshape(BLK, 128) for half in range(2)], axis=1)

    state = {}

    def invert():
        scales = []
        for which in range(2):
            rows = [jnp.sum(diags[w, :, :, which, :].reshape(16, 128), axis=0, keepdims=True) for w in range(8)]
            scales.append([1.0 / jnp.concatenate(rows[2 * k : 2 * k + 2], axis=1) for k in range(count)])

        half = BLK // 2
        above = upper[:half, :half]
        mats, corners = [], []
        for k in range(count):
            block = factor(0, k, k)
            for which, turned in ((0, block), (1, block.T)):
                scaled = turned * scales[which][k]
                mats += [jnp.where(above, scaled[:half, :half], 0.0), jnp.where(above, scaled[half:, half:], 0.0)]
                corners.append(scaled[:half, half:])
        invs = unit_upper_inverses(mats)
        inner = [product(split(n), invs[2 * e + 1]) for e, n in enumerate(corners)]
        inner = [split(-product(invs[2 * e], split(n))) for e, n in enumerate(inner)]
        for k in range(count):
            for which in range(2):
                e = 2 * k + which
                for at, ref in enumerate((mh_ref, ml_ref)):
                    ref[which, k, :half, :half] = invs[2 * e][at]
                    ref[which, k, half:, half:] = invs[2 * e + 1][at]
                    ref[which, k, :half, half:] = inner[e][at]
                    ref[which, k, half:, :half] = jnp.zeros((half, half), BF16)

        state["scales"] = scales

    def unpack():
        odd = lax.axis_index("bulk") % 2 == 1
        group = lax.broadcasted_iota(jnp.int32, (8, 128), 1) // 16
        columns = []
        for w in range(16):
            tiles = [orbs[e % 2, 4 * (w % 2) + e // 2, w // 2] for e in range(8)]
            tiles = [jnp.where(odd, pltpu.roll(t, 64, 1), t) for t in tiles]
            strips = []
            for h in range(4):
                strip = jnp.zeros((8, 128), F32)
                for e in range(8):
                    moved = tiles[e] if e == h else pltpu.roll(tiles[e], (16 * (e - h)) % 128, 1)
                    strip = jnp.where(group == e, moved, strip)
                strips.append(strip)
            columns.append(jnp.concatenate(strips, axis=0))
        blocks = [jnp.concatenate(columns[2 * k : 2 * k + 2], axis=1) for k in range(2 * count)]
        left, right = blocks[:count], blocks[count:]
        state["columns"] = left, right

    finish = exchange_body(tri, couple, orb, diag, whole, diags, orbs, sent, first, diag_tile, diag_in, orb_in, local, send, recv, pack_work, invert, unpack)
    scales = state["scales"]
    left, right = state["columns"]
    for k in range(count):
        x = thin_product(left[k] * scales[0][k], mh_ref[0, k], ml_ref[0, k])
        out_ref[:, pl.ds(BLK * k, BLK)] = x
        for i in range(k + 1, count):
            left[i] = left[i] - thin_product(x, *split(factor(0, i, k)))
        for i in range(count):
            right[i] = right[i] - thin_product(x, *split(factor(1, i, k)))
    for k in range(count):
        x = thin_product(right[k] * scales[1][k], mh_ref[1, k], ml_ref[1, k])
        out_ref[:, pl.ds(panel + BLK * k, BLK)] = x
        for i in range(k + 1, count):
            right[i] = right[i] - thin_product(x, *split(factor(0, k, i)), transposed=True)


    finish()


SENDS, RECVS = 24, 110


def exchange(orbitals, triangles, coupling, diagonals):
    anywhere = pl.BlockSpec(memory_space=pl.ANY)
    vmem = pl.BlockSpec(memory_space=pltpu.VMEM)
    return pl.pallas_call(
        exchange_kernel,
        out_shape=jax.ShapeDtypeStruct((32, 2048), F32),
        in_specs=[anywhere] * 4,
        out_specs=vmem,
        scratch_shapes=[
            pltpu.VMEM((2, 2, NX, NY, NZ, 2, 8, 128), F32),
            pltpu.VMEM((NY, NZ, 2, 2, 128), F32),
            pltpu.VMEM((2, NZ, NY, 8, 128), F32),
            pltpu.VMEM((NY, NZ, 8, 128), F32),
            pltpu.VMEM((NY, NZ, 8, 128), F32),
            pltpu.VMEM((2, 128), F32),
            pltpu.VMEM((2, 8), F32),
            pltpu.VMEM((16, 4096), F32),
            pltpu.VMEM((2, 4, BLK, BLK), BF16),
            pltpu.VMEM((2, 4, BLK, BLK), BF16),
            pltpu.SemaphoreType.DMA((9,)),
            pltpu.SemaphoreType.DMA((SENDS,)),
            pltpu.SemaphoreType.DMA((RECVS,)),
        ],
        compiler_params=pltpu.CompilerParams(collective_id=0, has_side_effects=True, vmem_limit_bytes=62 << 20),
        name="exchange",
    )(triangles, coupling, orbitals, diagonals)


def per_device(orbitals, triangles, coupling, diagonals):
    return exchange(orbitals.T, triangles.T, coupling.T, diagonals)


def solution(mesh):
    return jax.shard_map(
        per_device,
        mesh=mesh,
        in_specs=(P("rep", "bulk"), P("rep", "bulk"), P("rep", "bulk"), P(None, "bulk")),
        out_specs=P(("rep", "bulk"), None),
        check_vma=False,
    )
```

time: 190 us -> 66.6 us (0.35)
  waiting for transfers between devices: 104 us -> 0 us
  Pallas kernels: 22.9 us -> 64.7 us
  blocking collectives: 32.5 us -> 0 us
  between operations: 13.5 us -> 0.01 us
  local copies, waits for them, and re-layouts: 14.1 us -> 1.67 us
  other arithmetic: 2.64 us -> 0 us
    all_gather x1 -> x0, waiting for transfers between devices: 104 us -> none  [per_device(): whole = lax.all_gather(mine, ('rep', 'bulk'))]
    pallas_call x1, Pallas kernels: 22.9 us -> 64.7 us  [exchange(): pl.pallas_call(exchange_kernel, out_shape=jax.ShapeDtypeStruct((32, 2048)...]
    all_to_all x1 -> x0, blocking collectives: 32.5 us -> none  [per_device(): lax.all_to_all(blocks, 'bulk', split_axis=0, concat_axis=2, tiled=True)]
    reshape x5 -> x0, local copies, waits for them, and re-layouts: 9.54 us -> none  [the longest x1 7.21 us: per_device(): couple = whole[:, :, 8:16].reshape(4, 1024, 256)]
  transfers between devices with their start and end apart: 1 -> 0, of which waited for: 1 -> 0; matrix products, arithmetic and copies ran while one was open for 3% -> 0% of each run, Pallas kernels for 0% -> 0%
where the time goes in v3:
time: 66.6 us; the launch traced here: 66.4 us
  Pallas kernels  64.7 us (97%)
  local copies, waits for them, and re-layouts  1.67 us (3%)
    pallas_call x1, Pallas kernels, exchange(): pl.pallas_call(exchange_kernel, out_shape=jax.ShapeDtypeStruct((32, 2048)...  64.7 us
    unnamed x1, local copies, waits for them, and re-layouts  1.67 us

profile of v3, /device:TPU:1, one launch (start us, length us, event | category | flops | bytes accessed | tf_op | source)
XLA Modules:
  0.0 66.4 jit_solution(16835241593264340812)
XLA Ops:
  0.0 64.7 %exchange.1 = f32[32,2048]{1,0:T(8,128)} custom-call(f32[8,256]{1,0:T(8,128)} %bitcast.4, f32[8,256]{1,0:T(8,128)} %bitcast.5, f32[16,4096]{1,0:T(8,128)} %bitcast.3, f32[2,8]{1,0:T(2,128)} %diag.1), custom_call_target="tpu_custom_call" | custom-call | tf_op jit(solution)/shard_map/exchange/pallas_call | solution.py:400
  64.7 1.7 %copy.6 = f32[32,2048]{1,0:T(8,128)} copy(f32[32,2048]{1,0:T(8,128)} %exchange.1) | data formatting | bytes 524288

commit v4 on v3

--- a/solution.py
+++ b/solution.py
@@ -1,4 +1,5 @@
 import functools
+import heapq
 
 import jax
 import jax.numpy as jnp
@@ -54,6 +55,7 @@
         parts = [split(p) for p in power]
         inv = [m + product(split(m), p) for m, p in zip(inv, parts)]
         span *= 2
+        yield None
     width = BASE
     while width < size:
         corner = ((row // width) % 2 == 0) & ((col // width) == (row // width) + 1)
@@ -61,11 +63,22 @@
         corners = [product(split(jnp.where(corner, n, 0.0)), m) for n, m in zip(mats, parts)]
         inv = [m - product(ms, split(c)) for m, ms, c in zip(inv, parts, corners)]
         width *= 2
-    return [split(m) for m in inv]
-
-
-def ring_hops(n):
-    return [(1, d) for d in range(1, n // 2 + 1)] + [(-1, d) for d in range(1, n - n // 2)]
+        yield None
+    yield [split(m) for m in inv]
+
+
+def ring_plan(n, kind):
+    ahead, back = range(1, n // 2 + 1), range(1, n - n // 2)
+    if kind == 0:
+        step = {1: 0, 2: 1, 3: 2, 4: 3}
+    elif kind == 1:
+        step = {1: 0, 2: 0, 3: 2, 4: 2}
+    parent = {e: step[e] for e in ahead}
+    parent.update({-e: -step[e] for e in back})
+    rank = {0: 0}
+    for e in sorted(parent, key=abs):
+        rank[e] = rank[parent[e]] + 1
+    return parent, rank
 
 
 def exchange_body(tri, couple, orb, diag, whole, diags, orbs, sent, first, diag_tile, diag_in, orb_in, local, send, recv, pack_work, invert, unpack):
@@ -76,7 +89,7 @@
     s = 1 - 2 * c
     me = {"x": x, "y": y, "z": z}
     size = {"x": NX, "y": NY, "z": NZ}
-    used = {"send": 0, "recv": 0}
+    used = {"send": 0, "recv": 0, "order": 0, "now": 0}
 
     def new(kind):
         used[kind] += 1
@@ -119,21 +132,24 @@
     line_send = new("send")
     line_recv = {(t, half): new("recv") for t in range(2) for half in range(2)}
     order = (4, 3, 5, 2, 6, 1, 7)
-    for t, ref in ((1, couple), (0, tri)):
-        for o in order:
-            for half, axis in ((0, "z"), (1, "y")):
-                put(ref.at[:, pl.ds(128 * half, 128)], whole.at[t, half, x, y, z, c], device(axis, o), line_send, line_recv[t, half])
+    for o in order:
+        for half, axis in ((0, "z"), (1, "y")):
+            put(couple.at[:, pl.ds(128 * half, 128)], whole.at[1, half, x, y, z, c], device(axis, o), line_send, line_recv[1, half])
+    for o in (2, 1, 3):
+        for half in range(2):
+            put(tri.at[:, pl.ds(128 * half, 128)], whole.at[0, half, x, y, z, c], device("x", o), line_send, line_recv[0, half])
 
     pack_work(get_orb, get_diag)
     put_diag = pltpu.make_async_copy(diag_tile, diags.at[y, z, c], local.at[6])
     put_diag.start()
-    keep_first = pltpu.make_async_copy(sent.at[y], first.at[y], local.at[7])
+    own_line = lax.select(c == 0, y, z)
+    keep_first = pltpu.make_async_copy(sent.at[own_line], first.at[own_line], local.at[7])
     keep_first.start()
     diag_send, diag_recv = new("send"), new("recv")
     for o in order:
         put(diag_tile, diags.at[y, z, c], device("z", o), diag_send, diag_recv)
 
-    colours = [(1, 0, "z", "y", "x"), (1, 1, "y", "z", "x"), (0, 0, "z", "x", "y"), (0, 1, "y", "x", "z")]
+    colours = [(1, 0, "z", "y", "x"), (1, 1, "y", "z", "x"), (0, 0, "x", "z", "y"), (0, 1, "x", "y", "z")]
     ring_send = {colour: (new("send"), new("send")) for colour in colours}
     cross_send = new("send")
     cross_recv = {colour: new("recv") for colour in colours}
@@ -144,14 +160,17 @@
         at[line] = slice(None)
         return whole.at[t, half, at["x"], at["y"], at["z"], c]
 
-    def blocks_like(n):
-        a = {1: (1, 1), 2: (2, 1), 7: (1, 7), 3: (3, 1), 24: (3, 8), 28: (4, 7), 32: (4, 8)}[n]
-        return whole.at[0, 0, pl.ds(0, a[0]), pl.ds(0, a[1]), :, 0]
-
-    events = {}
-
-    def later(slot, action, rank=0):
-        events.setdefault(slot, []).append((rank, len(events.get(slot, [])), action))
+    def tiles_like(n):
+        for a in (4, 3, 2, 1):
+            for b in range(8, 0, -1):
+                if n % (a * b) == 0 and n // (a * b) <= 8:
+                    return whole.at[0, 0, pl.ds(0, a), pl.ds(0, b), pl.ds(0, n // (a * b)), 0]
+
+    events = []
+
+    def later(time, action):
+        heapq.heappush(events, (time, len(events) + used["order"], action))
+        used["order"] += 1000
 
     crossings = []
 
@@ -161,68 +180,76 @@
 
     def final_ring(colour, indices, slot):
         axis = colour[4]
-        n, hops = size[axis], ring_hops(size[axis])
-        sems = {hop: new("recv") for hop in hops}
-        for index in indices:
-            own = block(colour, index)
-            for way in (1, -1):
-                put(own, own, device(axis, way * s), ring_send[colour][1], sems[way, 1])
-            to_partner(colour, own)
-        for way, d in sorted(hops, key=lambda h: h[1]):
-            def action(way=way, d=d):
-                take(recv.at[sems[way, d]], blocks_like(len(indices)))
-                for index in indices:
-                    ref = block(colour, {**index, axis: shifted(axis, -way * s * d)})
-                    if (way, d + 1) in hops:
-                        put(ref, ref, device(axis, way * s), ring_send[colour][1], sems[way, d + 1])
-                    to_partner(colour, ref)
-            later(slot + d, action, 1)
+        kind = 0 if axis == "x" else 1
+        parent, rank = ring_plan(size[axis], kind)
+        sems = {e: new("recv") for e in parent}
+
+        def pass_on(e):
+            for index in indices:
+                ref = block(colour, {**index, axis: shifted(axis, -s * e)})
+                for f in parent:
+                    if parent[f] == e and f != e:
+                        put(ref, ref, device(axis, s * (f - e)), ring_send[colour][1], sems[f])
+                to_partner(colour, ref)
+
+        def action(e):
+            take(recv.at[sems[e]], tiles_like(size[colour[2]] * len(indices)))
+            pass_on(e)
+
+        pass_on(0)
+        for e in parent:
+            if axis == "x":
+                when = 20 + 40 * slot + 25 * rank[e]
+            else:
+                when = 5 + 30 * slot + 34 * rank[e]
+            later(max(when, used["now"] + 1), functools.partial(action, e))
 
     def middle_ring(colour):
         axis = colour[3]
-        n, hops = size[axis], ring_hops(size[axis])
-        sems = {hop: new("recv") for hop in hops}
-        own = block(colour, {})
-        for way in (1, -1):
-            put(own, own, device(axis, way * s), ring_send[colour][0], sems[way, 1])
-        for d in range(1, n // 2 + 1):
-            ways = [way for way in (1, -1) if (way, d) in hops]
-            def action(d=d, ways=ways):
-                indices = []
-                for way in ways:
-                    take(recv.at[sems[way, d]], blocks_like(1))
-                    index = {axis: shifted(axis, -way * s * d)}
-                    ref = block(colour, index)
-                    if (way, d + 1) in hops:
-                        put(ref, ref, device(axis, way * s), ring_send[colour][0], sems[way, d + 1])
-                    indices.append(index)
-                final_ring(colour, indices, d)
-            later(d, action)
-
-    for keep in keeps:
-        keep.wait()
-    for colour in colours:
-        take(recv.at[line_recv[colour[0], colour[1]]], whole.at[0, 0, 0, 0, pl.ds(0, 7), 0])
-        middle_ring(colour)
-    for colour in colours:
-        final_ring(colour, [{}], 0)
+        parent, rank = ring_plan(size[axis], 0 if axis == "x" else 1)
+        sems = {e: new("recv") for e in parent}
+
+        def pass_on(e):
+            ref = block(colour, {axis: shifted(axis, -s * e)})
+            for f in parent:
+                if parent[f] == e:
+                    put(ref, ref, device(axis, s * (f - e)), ring_send[colour][0], sems[f])
+
+        def action(es):
+            for e in es:
+                take(recv.at[sems[e]], tiles_like(size[colour[2]]))
+                pass_on(e)
+            indices = [{axis: shifted(axis, -s * e)} for e in es]
+            final_ring(colour, indices, rank[es[0]])
+
+        pass_on(0)
+        for r in range(1, max(rank.values()) + 1):
+            later((25 if colour[4] == "x" else 27) * r, functools.partial(action, [e for e in parent if rank[e] == r]))
 
     first_send, first_recv, second_send, second_recv = new("send"), new("recv"), new("send"), new("recv")
     dblock_send, dblock_recv = new("send"), new("recv")
     cross_small = [(new("send"), new("recv")) for _ in range(2)]
 
+    one = lax.select(c == 0, y, z)
+    two = lax.select(c == 0, z, y)
+
+    def crossing_device(first_axis, by):
+        along_y = lax.select(c == 0, by if first_axis else 0, 0 if first_axis else by)
+        along_z = by - along_y
+        at_y, at_z = lax.rem(y + along_y, NY), lax.rem(z + along_z, NZ)
+        return ((at_y * NZ + at_z) * 2 + c, x)
+
     def orbital_first():
+        for o in order:
+            put(sent.at[lax.rem(one + o, 8)], first.at[one], crossing_device(True, o), first_send, first_recv)
+
+    def orbital_second():
         keep_first.wait()
-        for o in order:
-            at = shifted("y", o)
-            put(sent.at[at], first.at[y], device("y", o), first_send, first_recv)
-
-    def orbital_second():
         take(recv.at[first_recv], first.at[pl.ds(0, 7)])
-        keep_second = pltpu.make_async_copy(first.at[:, z], orbs.at[c, z], local.at[8])
+        keep_second = pltpu.make_async_copy(first.at[:, two], orbs.at[c, two], local.at[8])
         keep_second.start()
         for o in order:
-            put(first.at[:, shifted("z", o)], orbs.at[c, z], device("z", o), second_send, second_recv)
+            put(first.at[:, lax.rem(two + o, 8)], orbs.at[c, two], crossing_device(False, o), second_send, second_recv)
         keep_second.wait()
 
     def orbital_last():
@@ -239,42 +266,55 @@
         take(recv.at[dblock_recv], diags.at[pl.ds(0, 7), :, 0])
         put(diags.at[:, :, c], diags.at[:, :, c], partner, *cross_small[1])
 
-    later(0, orbital_first, 2)
-    later(2, orbital_second, 2)
-    later(5, orbital_last, 2)
-    later(1, diag_second, 2)
-    later(3, diag_last, 2)
+    for keep in keeps:
+        keep.wait()
+    orbital_first()
+    for colour in colours:
+        take(recv.at[line_recv[colour[0], colour[1]]], tiles_like(size[colour[2]] - 1))
+        middle_ring(colour)
+    for colour in colours[:2]:
+        final_ring(colour, [{}], 0)
+    for colour in colours[2:]:
+        final_ring(colour, [{}], 0)
+
+    later(45, orbital_second)
+    later(110, orbital_last)
+    later(40, diag_second)
+    later(90, diag_last)
+
     def triangles_ready():
         take(recv.at[cross_small[1][1]], diags.at[:, :, 0])
         for colour in colours[2:]:
-            take(recv.at[cross_recv[colour]], blocks_like(32))
-        invert()
+            take(recv.at[cross_recv[colour]], tiles_like(256))
+        steps = invert()
+
+        def advance():
+            if next(steps, steps) is not steps:
+                later(used["now"] + 1, advance)
+
+        advance()
 
     def orbitals_ready():
         take(recv.at[cross_small[0][1]], orbs.at[0])
         unpack()
 
-    later(6, triangles_ready, 5)
-    later(6, orbitals_ready, 6)
-    slot = 0
-    while slot <= max(events):
-        done = 0
-        while done < len(events.get(slot, [])):
-            todo = sorted(events[slot][done:])
-            done += len(todo)
-            for _, _, action in todo:
-                action()
-        slot += 1
+    later(134, triangles_ready)
+    later(134 + 1, orbitals_ready)
+    while events:
+        time, _, action = heapq.heappop(events)
+        used["now"] = time
+        action()
 
     for colour in colours[:2]:
-        take(recv.at[cross_recv[colour]], blocks_like(32))
+        take(recv.at[cross_recv[colour]], tiles_like(256))
 
     def finish():
-        take(send.at[line_send], whole.at[:, :, 0, 0, pl.ds(0, 7), 0])
+        take(send.at[line_send], tiles_like(20))
         take(send.at[diag_send], diags.at[0, pl.ds(0, 7), 0])
         for colour in colours:
-            take(send.at[ring_send[colour][0]], blocks_like(7 if size[colour[3]] == 8 else 3))
-            take(send.at[ring_send[colour][1]], blocks_like(24 if size[colour[4]] == 4 else 28))
+            per, middle, last = (size[axis] for axis in colour[2:])
+            take(send.at[ring_send[colour][0]], tiles_like(per * (middle - 1)))
+            take(send.at[ring_send[colour][1]], tiles_like(per * middle * (last - 1)))
         take(send.at[cross_send], whole.at[:, :, :, :, :, 0])
         take(send.at[first_send], first.at[pl.ds(0, 7)])
         take(send.at[second_send], orbs.at[0, pl.ds(0, 7)])
@@ -282,12 +322,13 @@
         take(send.at[cross_small[0][0]], orbs.at[0])
         take(send.at[cross_small[1][0]], diags.at[:, :, 0])
 
-    assert used["send"] <= SENDS and used["recv"] <= RECVS, used
+    assert used["send"] <= SENDS and used["recv"] <= RECVS
     return finish
 
 
 def pack_into(orb_in, diag_in, sent, diag_tile):
     place = lax.axis_index("bulk") % 16
+    odd = lax.axis_index("bulk") % 2 == 1
     lane = lax.broadcasted_iota(jnp.int32, (2, 128), 1)
     spread = jnp.concatenate([diag_in[...]] * 16, axis=1)
     diag_tile[...] = jnp.where(lane // 8 == place, spread, 0.0)
@@ -303,7 +344,7 @@
                     moved = pieces[h] if h == t else pltpu.roll(pieces[h], (16 * (h - t)) % 128, 1)
                     tile = jnp.where(group == h, moved, tile)
                 chip = 2 * (8 * g + t) + p
-                sent[chip // NZ, chip % NZ] = tile
+                sent[lax.select(odd, chip % NZ, chip // NZ), lax.select(odd, chip // NZ, chip % NZ)] = tile
 
 
 def exchange_kernel(tri, couple, orb, diag, out_ref, whole, diags, orbs, sent, first, diag_tile, diag_in, orb_in, mh_ref, ml_ref, local, send, recv):
@@ -338,7 +379,8 @@
                 scaled = turned * scales[which][k]
                 mats += [jnp.where(above, scaled[:half, :half], 0.0), jnp.where(above, scaled[half:, half:], 0.0)]
                 corners.append(scaled[:half, half:])
-        invs = unit_upper_inverses(mats)
+        for invs in unit_upper_inverses(mats):
+            yield
         inner = [product(split(n), invs[2 * e + 1]) for e, n in enumerate(corners)]
         inner = [split(-product(invs[2 * e], split(n))) for e, n in enumerate(inner)]
         for k in range(count):
@@ -357,7 +399,8 @@
         group = lax.broadcasted_iota(jnp.int32, (8, 128), 1) // 16
         columns = []
         for w in range(16):
-            tiles = [orbs[e % 2, 4 * (w % 2) + e // 2, w // 2] for e in range(8)]
+            places = [(4 * (w % 2) + e // 2, w // 2) for e in range(8)]
+            tiles = [orbs[1, py, pz] if e % 2 else orbs[0, pz, py] for e, (pz, py) in enumerate(places)]
             tiles = [jnp.where(odd, pltpu.roll(t, 64, 1), t) for t in tiles]
             strips = []
             for h in range(4):
@@ -391,7 +434,7 @@
     finish()
 
 
-SENDS, RECVS = 24, 110
+SENDS, RECVS = 24, 112
 
 
 def exchange(orbitals, triangles, coupling, diagonals):

time: 66.6 us -> 59.6 us (0.89)
  Pallas kernels: 64.7 us -> 57.8 us
    pallas_call x1, Pallas kernels: 64.7 us -> 57.8 us  [exchange(): pl.pallas_call(exchange_kernel, out_shape=jax.ShapeDtypeStruct((32, 2048)...]
where the time goes in v4:
time: 59.6 us; the launch traced here: 59.5 us
  Pallas kernels  57.8 us (97%)
  local copies, waits for them, and re-layouts  1.67 us (3%)
    pallas_call x1, Pallas kernels, exchange(): pl.pallas_call(exchange_kernel, out_shape=jax.ShapeDtypeStruct((32, 2048)...  57.8 us
    unnamed x1, local copies, waits for them, and re-layouts  1.67 us

profile of v4, /device:TPU:1, one launch (start us, length us, event | category | flops | bytes accessed | tf_op | source)
XLA Modules:
  0.0 59.5 jit_solution(14670300470788605606)
XLA Ops:
  0.0 57.8 %exchange.1 = f32[32,2048]{1,0:T(8,128)} custom-call(f32[8,256]{1,0:T(8,128)} %bitcast.4, f32[8,256]{1,0:T(8,128)} %bitcast.5, f32[16,4096]{1,0:T(8,128)} %bitcast.3, f32[2,8]{1,0:T(2,128)} %diag.1), custom_call_target="tpu_custom_call" | custom-call | tf_op jit(solution)/shard_map/exchange/pallas_call | solution.py:443
  57.8 1.7 %copy.6 = f32[32,2048]{1,0:T(8,128)} copy(f32[32,2048]{1,0:T(8,128)} %exchange.1) | data formatting | bytes 524288

commit v5 on v4

--- a/solution.py
+++ b/solution.py
@@ -81,7 +81,7 @@
     return parent, rank
 
 
-def exchange_body(tri, couple, orb, diag, whole, diags, orbs, sent, first, diag_tile, diag_in, orb_in, local, send, recv, pack_work, invert, unpack):
+def exchange_body(tri, couple, orb, diag, whole, diags, orbs, sent, first, diag_tile, diag_in, orb_in, local, send, recv, pack_work, invert, unpack, solve_left, subtract):
     bulk, x = lax.axis_index("bulk"), lax.axis_index("rep")
     c = lax.rem(bulk, 2)
     z = lax.rem(bulk // 2, NZ)
@@ -299,14 +299,16 @@
         unpack()
 
     later(134, triangles_ready)
-    later(134 + 1, orbitals_ready)
+    later(136, orbitals_ready)
     while events:
         time, _, action = heapq.heappop(events)
         used["now"] = time
         action()
 
+    solve_left()
     for colour in colours[:2]:
         take(recv.at[cross_recv[colour]], tiles_like(256))
+        subtract(colour[1])
 
     def finish():
         take(send.at[line_send], tiles_like(20))
@@ -414,16 +416,31 @@
         left, right = blocks[:count], blocks[count:]
         state["columns"] = left, right
 
-    finish = exchange_body(tri, couple, orb, diag, whole, diags, orbs, sent, first, diag_tile, diag_in, orb_in, local, send, recv, pack_work, invert, unpack)
+    def solve_left():
+        scales = state["scales"]
+        left, _ = state["columns"]
+        solved = []
+        for k in range(count):
+            x = thin_product(left[k] * scales[0][k], mh_ref[0, k], ml_ref[0, k])
+            out_ref[:, pl.ds(BLK * k, BLK)] = x
+            solved.append(x)
+            for i in range(k + 1, count):
+                left[i] = left[i] - thin_product(x, *split(factor(0, i, k)))
+        state["solved"] = jnp.concatenate(solved, axis=1)
+        state["updates"] = {}
+
+    def subtract(half):
+        for pair in range(count // 2):
+            both = jnp.concatenate([whole[1, half, 2 * pair + e].reshape(panel, 128) for e in range(2)], axis=1)
+            update = thin_product(state["solved"], *split(both))
+            for e in range(2):
+                state["updates"][half, 2 * pair + e] = update[:, 128 * e : 128 * e + 128]
+
+    finish = exchange_body(tri, couple, orb, diag, whole, diags, orbs, sent, first, diag_tile, diag_in, orb_in, local, send, recv, pack_work, invert, unpack, solve_left, subtract)
     scales = state["scales"]
-    left, right = state["columns"]
-    for k in range(count):
-        x = thin_product(left[k] * scales[0][k], mh_ref[0, k], ml_ref[0, k])
-        out_ref[:, pl.ds(BLK * k, BLK)] = x
-        for i in range(k + 1, count):
-            left[i] = left[i] - thin_product(x, *split(factor(0, i, k)))
-        for i in range(count):
-            right[i] = right[i] - thin_product(x, *split(factor(1, i, k)))
+    _, right = state["columns"]
+    updates = state["updates"]
+    right = [right[i] - jnp.concatenate([updates[0, i], updates[1, i]], axis=1) for i in range(count)]
     for k in range(count):
         x = thin_product(right[k] * scales[1][k], mh_ref[1, k], ml_ref[1, k])
         out_ref[:, pl.ds(panel + BLK * k, BLK)] = x

time: 59.6 us -> 60.2 us (1.010)
  no operation moved by 1% of the time
where the time goes in v5:
time: 60.2 us; the launch traced here: 60.1 us
  Pallas kernels  58.4 us (97%)
  local copies, waits for them, and re-layouts  1.67 us (3%)
    pallas_call x1, Pallas kernels, exchange(): pl.pallas_call(exchange_kernel, out_shape=jax.ShapeDtypeStruct((32, 2048)...  58.4 us
    unnamed x1, local copies, waits for them, and re-layouts  1.67 us

profile of v5, /device:TPU:1, one launch (start us, length us, event | category | flops | bytes accessed | tf_op | source)
XLA Modules:
  0.0 60.1 jit_solution(3590052829729262660)
XLA Ops:
  0.0 58.4 %exchange.1 = f32[32,2048]{1,0:T(8,128)} custom-call(f32[8,256]{1,0:T(8,128)} %bitcast.4, f32[8,256]{1,0:T(8,128)} %bitcast.5, f32[16,4096]{1,0:T(8,128)} %bitcast.3, f32[2,8]{1,0:T(2,128)} %diag.1), custom_call_target="tpu_custom_call" | custom-call | tf_op jit(solution)/shard_map/exchange/pallas_call | solution.py:460
  58.4 1.7 %copy.6 = f32[32,2048]{1,0:T(8,128)} copy(f32[32,2048]{1,0:T(8,128)} %exchange.1) | data formatting | bytes 524288
